TPU v7x, 512 devices: a whole 4x4x16 slice. The times are simulated.
512 devices in a mesh: dp: 2 (over z_hi), fsdp: 16 (over z_lo, core), tile: 16 (over y, x).
Axes of the slice: x: 4, y: 4, z: 16 (z_hi: 2, z_lo: 8; z = z_hi * 8 + z_lo), core: 2. Of those that a mesh axis runs over, the one named last changes fastest.
Arguments:
- tokens: bfloat16 [32, 8, 512, 1536], P(('dp', 'fsdp'), None, 'tile'), may hold values from -6 to 6
- norm_gain: float32 [1536], replicated, may hold values from 0.25 to 1.75
- query_key_value_weight: bfloat16 [1536, 2304], P('fsdp'), may hold values from -5 to 5
- out_weight: bfloat16 [768, 1536], P('fsdp'), may hold values from -0.21875 to 0.21875
- head_weight: bfloat16 [1536, 320], P('fsdp'), may hold values from -0.15625 to 0.15625
- coarse: float32 [32, 20, 8, 512], P(('dp', 'fsdp'), None, None, 'tile'), may hold values from -36 to 36
- grad_fine: float32 [32, 20, 32, 2048], P(('dp', 'fsdp'), None, None, 'tile'), may hold values from -0.6 to 0.6
Outputs:
- fine_grid: float32 [32, 20, 32, 2048], P(('dp', 'fsdp'), None, None, 'tile')
- grad_tokens: bfloat16 [32, 8, 512, 1536], P(('dp', 'fsdp'), None, 'tile')
- grad_head: float32 [1536, 320], P('fsdp')
All inputs are finite; a program needn't handle non-finite values.
Results may differ from a plain program's by a relative error of at most 0.0059.
Values may be sent and summed in bfloat16 or wider, within the bound.
No kernel may reach another device: no remote copies, remote signals or barrier semaphores. Data moves between devices by JAX's collectives and lax.ppermute only.
A program may use at most 64 MiB of HBM per device.

v0:
```python
import jax
import jax.numpy as jnp
from jax import lax
from jax.sharding import PartitionSpec as P

D = 1536
HEADS = 8
HEAD_DIM = 96
VARS = 20
MARGIN = 8
INNER = 768
HEAD_OUT = 320
EPSILON = 1e-05


def with_halo(shard, sides, width):
    for axis, dim in sides:
        devices, length = (lax.axis_size(axis), shard.shape[dim])
        up = [(i, (i + 1) % devices) for i in range(devices)]
        down = [(j, i) for i, j in up]
        last = lax.slice_in_dim(shard, length - width, length, axis=dim)
        leading = lax.slice_in_dim(shard, 0, width, axis=dim)
        before = lax.ppermute(last, axis, up)
        after = lax.ppermute(leading, axis, down)
        shard = jnp.concatenate([before, shard, after], axis=dim)
    return shard


def from_behind(value, axis, steps):
    count = lax.axis_size(axis)
    pairs = [(source, (source + steps) % count) for source in range(count)]
    return lax.ppermute(value, axis, pairs)


def layer_norm(values):
    average = jnp.mean(values, axis=-1, keepdims=True)
    centred = values - average
    variance = jnp.mean(centred * centred, axis=-1, keepdims=True)
    inverse_dev = lax.rsqrt(variance + EPSILON)
    return (centred * inverse_dev, inverse_dev)


def norm_backward(grad_normed, standard, inverse_dev, norm_gain):
    grad_standard = grad_normed * norm_gain
    first_mean = jnp.mean(grad_standard, axis=-1, keepdims=True)
    second_mean = jnp.mean(grad_standard * standard, axis=-1, keepdims=True)
    return inverse_dev * (grad_standard - first_mean - standard * second_mean)


def attend_forward(queries, keys_values):
    query_count = queries.shape[0]
    key_count = keys_values.shape[0]
    score_scale = HEAD_DIM ** (-0.5)
    query_heads = queries.reshape(query_count, HEADS, HEAD_DIM)
    key_heads = keys_values[:, :INNER].reshape(key_count, HEADS, HEAD_DIM)
    value_heads = keys_values[:, INNER:].reshape(key_count, HEADS, HEAD_DIM)
    scores = (
        jnp.einsum("qhd,khd->hqk", query_heads, key_heads, preferred_element_type=jnp.float32)
        * score_scale
    )
    biggest = jnp.max(scores, axis=-1, keepdims=True)
    exponent = jnp.exp(scores - biggest)
    softmax_out = exponent / jnp.sum(exponent, axis=-1, keepdims=True)
    softmax_low = softmax_out.astype(jnp.bfloat16)
    attended = jnp.einsum(
        "hqk,khd->qhd", softmax_low, value_heads, preferred_element_type=jnp.float32
    )
    return (attended.astype(jnp.bfloat16).reshape(query_count, INNER), softmax_out)


def attend_backward(softmax_out, queries, keys_values, grad_attended):
    query_count = queries.shape[0]
    key_count = keys_values.shape[0]
    score_scale = HEAD_DIM ** (-0.5)
    query_heads = queries.reshape(query_count, HEADS, HEAD_DIM)
    key_heads = keys_values[:, :INNER].reshape(key_count, HEADS, HEAD_DIM)
    value_heads = keys_values[:, INNER:].reshape(key_count, HEADS, HEAD_DIM)
    grad_heads = grad_attended.reshape(query_count, HEADS, HEAD_DIM)
    softmax_low = softmax_out.astype(jnp.bfloat16)
    grad_values = jnp.einsum(
        "hqk,qhd->khd", softmax_low, grad_heads, preferred_element_type=jnp.float32
    )
    grad_weights = jnp.einsum(
        "qhd,khd->hqk", grad_heads, value_heads, preferred_element_type=jnp.float32
    )
    weighted = jnp.sum(softmax_out * grad_weights, axis=-1, keepdims=True)
    grad_scores = (softmax_out * (grad_weights - weighted)).astype(jnp.bfloat16)
    grad_queries = (
        jnp.einsum("hqk,khd->qhd", grad_scores, key_heads, preferred_element_type=jnp.float32)
        * score_scale
    )
    grad_keys = (
        jnp.einsum("hqk,qhd->khd", grad_scores, query_heads, preferred_element_type=jnp.float32)
        * score_scale
    )
    pair_gradient_rows = jnp.concatenate(
        [grad_keys.reshape(key_count, INNER), grad_values.reshape(key_count, INNER)], axis=1
    )
    return (grad_queries.astype(jnp.bfloat16).reshape(query_count, INNER), pair_gradient_rows)


def interp_weights(fine_index):
    coarse_cell = fine_index // 4
    phase_index = fine_index % 4
    lower_shift = (phase_index < 2).astype(jnp.int32)
    upper_weight = (2 * phase_index - 3 + 8 * lower_shift).astype(jnp.float32) / 8.0
    return (coarse_cell - lower_shift, upper_weight)


def build_matrix(lower_cell, upper_cell, upper_weight, count):
    columns = jnp.arange(count, dtype=jnp.int32)
    lower_part = jnp.where(
        columns[None, :] == lower_cell[:, None], 1.0 - upper_weight[:, None], 0.0
    )
    upper_portion = jnp.where(columns[None, :] == upper_cell[:, None], upper_weight[:, None], 0.0)
    return lower_part + upper_portion


def contract_last(left_side, right_side):
    return lax.dot_general(
        left_side, right_side, (((1,), (1,)), ((), ())), preferred_element_type=jnp.float32
    )


def shards(tokens, norm_gain, query_key_value_weight, out_weight, head_weight, coarse, grad_fine):
    lat_rows = tokens.shape[1]
    lon_cols = tokens.shape[2]
    row_count = lat_rows * lon_cols
    flattened_rows = tokens[0].reshape(row_count, D).astype(jnp.float32)
    standard, inverse_dev = layer_norm(flattened_rows)
    normed = (standard * norm_gain).astype(jnp.bfloat16)
    full_qkv = lax.all_gather(query_key_value_weight, "fsdp", axis=0, tiled=True)
    projected = jnp.dot(normed, full_qkv, preferred_element_type=jnp.float32).astype(jnp.bfloat16)
    queries = projected[:, :INNER]
    pairs_local = projected[:, INNER:]
    margin_pairs = with_halo(
        pairs_local.reshape(lat_rows, lon_cols, 2 * INNER), (("tile", 1),), MARGIN
    )
    keys_values = margin_pairs.reshape(lat_rows * (lon_cols + 2 * MARGIN), 2 * INNER)
    attended, softmax_out = attend_forward(queries, keys_values)
    full_out = lax.all_gather(out_weight, "fsdp", axis=0, tiled=True)
    mixed_out = jnp.dot(attended, full_out, preferred_element_type=jnp.float32)
    hidden = (flattened_rows + mixed_out).astype(jnp.bfloat16)
    full_head = lax.all_gather(head_weight, "fsdp", axis=0, tiled=True)
    head_out = jnp.dot(hidden, full_head, preferred_element_type=jnp.float32)
    fine_head = (
        head_out.reshape(lat_rows, lon_cols, VARS, 4, 4)
        .transpose(2, 0, 3, 1, 4)
        .reshape(VARS, 4 * lat_rows, 4 * lon_cols)
    )
    coarse_padded_grid = with_halo(coarse[0], (("tile", 2),), 1)
    lat_lower, lat_upper_weight = interp_weights(jnp.arange(4 * lat_rows, dtype=jnp.int32))
    latitude_matrix = build_matrix(
        jnp.clip(lat_lower, 0, lat_rows - 1),
        jnp.clip(lat_lower + 1, 0, lat_rows - 1),
        lat_upper_weight,
        lat_rows,
    )
    lon_lower, lon_upper_weight = interp_weights(jnp.arange(4 * lon_cols, dtype=jnp.int32))
    lon_matrix = build_matrix(lon_lower + 1, lon_lower + 2, lon_upper_weight, lon_cols + 2)
    incomplete_grid = jnp.einsum(
        "lj,kji->kli", latitude_matrix, coarse_padded_grid, precision=lax.Precision.HIGHEST
    )
    residual = jnp.einsum(
        "vrb,cb->vrc", incomplete_grid, lon_matrix, precision=lax.Precision.HIGHEST
    )
    fine_grid = fine_head + residual
    grad_rows = (
        grad_fine[0]
        .reshape(VARS, lat_rows, 4, lon_cols, 4)
        .transpose(1, 3, 0, 2, 4)
        .reshape(row_count, HEAD_OUT)
    )
    grad_rows = grad_rows.astype(jnp.bfloat16)
    head_term = lax.dot_general(
        hidden, grad_rows, (((0,), (0,)), ((), ())), preferred_element_type=jnp.float32
    )
    head_block = lax.psum_scatter(head_term, "fsdp", scatter_dimension=0, tiled=True)
    grad_head = lax.psum(head_block, ("dp", "tile"))
    grad_hidden = contract_last(grad_rows, full_head)
    grad_attended = contract_last(grad_hidden.astype(jnp.bfloat16), full_out).astype(jnp.bfloat16)
    grad_queries, pair_gradient_rows = attend_backward(
        softmax_out, queries, keys_values, grad_attended
    )
    pair_gradient_rows = pair_gradient_rows.reshape(lat_rows, lon_cols + 2 * MARGIN, 2 * INNER)
    from_left = from_behind(pair_gradient_rows[:, lon_cols + MARGIN :], "tile", 1)
    from_right = from_behind(pair_gradient_rows[:, :MARGIN], "tile", -1)
    own_cells = pair_gradient_rows[:, MARGIN : MARGIN + lon_cols]
    own_cells = own_cells + jnp.pad(from_left, ((0, 0), (0, lon_cols - MARGIN), (0, 0)))
    own_cells = own_cells + jnp.pad(from_right, ((0, 0), (lon_cols - MARGIN, 0), (0, 0)))
    grad_all = jnp.concatenate(
        [grad_queries, own_cells.reshape(row_count, 2 * INNER).astype(jnp.bfloat16)], axis=1
    )
    grad_normed = contract_last(grad_all, full_qkv)
    grad_input = grad_hidden + norm_backward(grad_normed, standard, inverse_dev, norm_gain)
    grad_tokens = grad_input.astype(jnp.bfloat16).reshape(1, lat_rows, lon_cols, D)
    return (fine_grid[None], grad_tokens, grad_head)


def solution(mesh):
    placed = (
        P(("dp", "fsdp"), None, "tile", None),
        P(),
        P("fsdp", None),
        P("fsdp", None),
        P("fsdp", None),
        P(("dp", "fsdp"), None, None, "tile"),
        P(("dp", "fsdp"), None, None, "tile"),
    )
    return jax.shard_map(
        shards,
        mesh=mesh,
        in_specs=placed,
        out_specs=(
            P(("dp", "fsdp"), None, None, "tile"),
            P(("dp", "fsdp"), None, "tile", None),
            P("fsdp", None),
        ),
        check_vma=False,
    )
```

profile of v0, /device:TPU:2, one launch (start us, length us, event | category | flops | bytes accessed | tf_op | source)
XLA Modules:
  0.0 943.6 jit_solution(4857148850893295786)
XLA Ops:
  8.7 1.7 fusion.56
  10.4 3.4 collective-permute-start.2
  13.8 6.3 collective-permute-start.3
  20.1 1.3 convert_reduce_fusion
  22.5 1.5 copy.23
  24.0 1.1 convert_element_type.125
  25.7 46.6 %all_gather.11 = bf16[1536,320]{1,0:T(8,128)(2,1)S(1)} all-gather(bf16[96,320]{1,0:T(8,128)(2,1)} %param.11), channel_id=1, replica_groups=mesh['dp'=2,'fsdp'=16,'tile'=16] {'fsdp'}, dimensions={0}, use_global_device_ids=true | all-gather | bytes 1044480 | tf_op jit(solution)/shard_map/all_gather | solution.py:144
  72.3 1.6 fusion.59
  73.9 1.2 multiply_convert_fusion.1
  75.7 2.1 convolution_bitcast_fusion.1
  77.8 55.1 %all-gather.3.cloned.1.call-done = bf16[1536,2304]{1,0:T(8,128)(2,1)} async-done(((bf16[96,2304]{1,0:T(8,128)(2,1)}), bf16[1536,2304]{1,0:T(8,128)(2,1)}) %all-gather.3.cloned.1.call-update) | async-done | bytes 7077904 | tf_op jit(solution)/shard_map/all_gather | solution.py:132
  132.9 5.3 convolution_convert_fusion
  140.0 3.2 collective-permute-start
  143.2 2.8 collective-permute-start.1
  146.0 86.6 %all-gather.5.cloned.1.call-done = bf16[768,1536]{1,0:T(8,128)(2,1)} async-done(((bf16[48,1536]{1,0:T(8,128)(2,1)}), bf16[768,1536]{1,0:T(8,128)(2,1)}) %all-gather.5.cloned.1.call-update) | async-done | bytes 2359312 | tf_op jit(solution)/shard_map/all_gather | solution.py:141
  232.6 3.2 convolution_convert_fusion.1
  235.8 1.9 copy.24
  237.8 1.8 slice.50
  239.6 1.9 copy.18
  241.5 1.4 pad_maximum_fusion
  243.9 2.1 copy.29
  246.1 2.1 copy.28
  248.2 4.0 fusion.57
  252.2 2.9 convolution_convert_fusion.2
  256.0 1.3 fusion.58
  257.3 2.0 fusion.60
  259.3 1.4 reshape.187
  260.7 3.0 copy.20
  263.8 3.0 copy.21
  266.8 2.6 convolution_bitcast_fusion
  269.3 1.6 copy.26
  271.0 2.7 concatenate.20
  274.9 3.0 multiply_reduce_fusion
  278.6 1.1 copy-done.1
  280.2 1.7 copy.25
  281.9 1.9 concatenate.19
  285.2 1.5 copy-done.5
  287.6 3.4 collective-permute-start.4
  291.1 2.8 collective-permute-start.5
  295.5 1.1 fusion.11
  296.7 3.5 collective-permute-done.4
  300.2 3.3 collective-permute-done.5
  303.5 1.7 fusion.6
  305.2 6.3 fusion.52
  311.6 73.0 %reduce-scatter.2.cloned.1.call-done = f32[96,320]{1,0:T(8,128)} async-done(((f32[1536,320]{1,0:T(8,128)}), f32[96,320]{1,0:T(8,128)}) %reduce-scatter.2.cloned.1.call-update) | async-done | bytes 122896 | tf_op jit(solution)/shard_map/reduce_scatter | solution.py:178
  384.5 2.9 add_convert_fusion
  387.4 548.1 %all-reduce.4.cloned.1.call-done = f32[96,320]{1,0:T(8,128)} async-done(((f32[96,320]{1,0:T(8,128)}), f32[96,320]{1,0:T(8,128)}) %all-reduce.4.cloned.1.call-update) | async-done | bytes 122896 | tf_op jit(solution)/shard_map/psum | solution.py:179
  935.5 1.6 copy.32
  (85 shorter events, 13.8 us)
Async XLA Ops:
  7.2 14.4 %copy-start = (bf16[1,8,32,1536]{3,2,1,0:T(8,128)(2,1)S(1)}, bf16[1,8,32,1536]{3,2,1,0:T(8,128)(2,1)}, u32[]{:S(2)}) copy-start(bf16[1,8,32,1536]{3,2,1,0:T(8,128)(2,1)} %param.7) | copy-start | bytes 2359300
  7.2 14.8 %copy-start.19 = (f32[1,20,32,128]{3,2,1,0:T(8,128)S(1)}, f32[1,20,32,128]{3,2,1,0:T(8,128)}, u32[]{:S(2)}) copy-start(f32[1,20,32,128]{3,2,1,0:T(8,128)} %param.13) | copy-start | bytes 983044
  7.2 125.7 %all-gather.3.cloned.1.call-start = ((), (), s32[]{:S(2)}) async-start(), calls=%async_computation.1 | async-start | bytes 7520256 | tf_op jit(solution)/shard_map/all_gather | solution.py:132
  7.9 224.7 %all-gather.5.cloned.1.call-start = ((), (), s32[]{:S(2)}) async-start(), calls=%async_computation.2 | async-start | bytes 2506752 | tf_op jit(solution)/shard_map/all_gather | solution.py:141
  8.7 375.8 %reduce-scatter.2.cloned.1.call-start = ((), (), s32[]{:S(2)}) async-start(), calls=%async_computation.3 | async-start | bytes 2506752 | tf_op jit(solution)/shard_map/reduce_scatter | solution.py:178
  10.4 65.2 %collective-permute-start.2 = (f32[20,8,1]{2,1,0:T(8,128)}, f32[20,8,1]{2,1,0:T(8,128)}, u32[]{:S(2)}, u32[]{:S(2)}) collective-permute-start(f32[20,8,1]{2,1,0:T(8,128)} %get-tuple-element.11), channel_id=1, source_target_pairs={{0,1},{1,2},{2,3},{3,4},{4,5},{5,6},{6,7},{7,8},{8,9},{9,10},{10,1... | collective-permute-start | bytes 1928 | tf_op jit(solution)/shard_map/ppermute | solution.py:23
  13.8 61.8 %collective-permute-start.3 = (f32[20,8,1]{2,1,0:T(8,128)}, f32[20,8,1]{2,1,0:T(8,128)}, u32[]{:S(2)}, u32[]{:S(2)}) collective-permute-start(f32[20,8,1]{2,1,0:T(8,128)} %get-tuple-element.12), channel_id=1, source_target_pairs={{1,0},{2,1},{3,2},{4,3},{5,4},{6,5},{7,6},{8,7},{9,8},{10,9},{11,1... | collective-permute-start | bytes 1928 | tf_op jit(solution)/shard_map/ppermute | solution.py:24
  72.3 1.6 copy-start.20
  72.3 3.4 copy-start.15
  138.2 1.8 copy-start.14
  138.2 1.0 copy-start.7
  140.0 101.5 %collective-permute-start = (bf16[8,8,1536]{2,1,0:T(8,128)(2,1)}, bf16[8,8,1536]{2,1,0:T(8,128)(2,1)}, u32[]{:S(2)}, u32[]{:S(2)}) collective-permute-start(bf16[8,8,1536]{2,1,0:T(8,128)(2,1)} %get-tuple-element.9), channel_id=1, source_target_pairs={{0,1},{1,2},{2,3},{3,4},{4,5},{5,6},{6,7},{7,8},{8,9},{9,10},{10,1... | collective-permute-start | bytes 589832 | tf_op jit(solution)/shard_map/ppermute | solution.py:23
  143.2 98.3 %collective-permute-start.1 = (bf16[8,8,1536]{2,1,0:T(8,128)(2,1)}, bf16[8,8,1536]{2,1,0:T(8,128)(2,1)}, u32[]{:S(2)}, u32[]{:S(2)}) collective-permute-start(bf16[8,8,1536]{2,1,0:T(8,128)(2,1)} %get-tuple-element.10), channel_id=1, source_target_pairs={{1,0},{2,1},{3,2},{4,3},{5,4},{6,5},{7,6},{8,7},{9,8},{10,9},{11,1... | collective-permute-start | bytes 589832 | tf_op jit(solution)/shard_map/ppermute | solution.py:24
  252.2 2.9 copy-start.4
  256.0 1.3 copy-start.10
  257.3 2.0 copy-start.12
  273.7 1.1 copy-start.16
  273.7 1.2 copy-start.17
  273.7 661.8 %all-reduce.4.cloned.1.call-start = ((), (), s32[]{:S(2)}) async-start(), calls=%async_computation.4 | async-start | bytes 294912 | tf_op jit(solution)/shard_map/psum | solution.py:179
  274.9 3.0 copy-start.3
  277.9 1.9 copy-start.9
  278.6 1.2 copy-start.1
  283.8 1.3 copy-start.8
  285.0 8.9 copy-start.2
  285.0 8.9 copy-start.6
  285.2 1.5 copy-start.5
  287.6 12.6 %collective-permute-start.4 = (f32[8,8,1536]{2,1,0:T(8,128)}, f32[8,8,1536]{2,1,0:T(8,128)}, u32[]{:S(2)}, u32[]{:S(2)}) collective-permute-start(f32[8,8,1536]{2,1,0:T(8,128)} %get-tuple-element.5), channel_id=1, source_target_pairs={{0,1},{1,2},{2,3},{3,4},{4,5},{5,6},{6,7},{7,8},{8,9},{9,10},{10,1... | collective-permute-start | bytes 1179656 | tf_op jit(solution)/shard_map/ppermute | solution.py:32
  291.0 4.5 copy-start.11
  291.0 4.5 copy-start.13
  291.0 4.5 copy-start.22
  291.0 4.5 copy-start.23
  291.0 4.5 copy-start.24
  291.1 4.5 copy-start.25
  291.1 12.4 %collective-permute-start.5 = (f32[8,8,1536]{2,1,0:T(8,128)}, f32[8,8,1536]{2,1,0:T(8,128)}, u32[]{:S(2)}, u32[]{:S(2)}) collective-permute-start(f32[8,8,1536]{2,1,0:T(8,128)} %get-tuple-element.6), channel_id=1, source_target_pairs={{0,15},{1,0},{2,1},{3,2},{4,3},{5,4},{6,5},{7,6},{8,7},{9,8},{10,9... | collective-permute-start | bytes 1179656 | tf_op jit(solution)/shard_map/ppermute | solution.py:32
  296.7 8.5 copy-start.18
  296.7 8.6 copy-start.21
Sparse Core Ops, SparseCore 0:
  10.1 122.7 all-gather.2
  135.0 97.5 all-gather.4
  273.8 110.6 reduce-scatter.1
  387.3 548.2 all-reduce.3
where the time goes:
time: 945 us; the launch traced here: 944 us
  waiting for transfers between devices  771 us (82%)
  blocking collectives  46.6 us (5%)
  local copies, waits for them, and re-layouts  41.8 us (4%)
  matrix products  37.3 us (4%)
  starting transfers between devices  22.1 us (2%)
  between operations  14.2 us (2%)
  other arithmetic  10.8 us (1%)
    psum x1, waiting for transfers between devices, shards(): grad_head = lax.psum(head_block, ('dp', 'tile'))  548 us
    all_gather x1, waiting for transfers between devices, shards(): full_out = lax.all_gather(out_weight, 'fsdp', axis=0, tiled=True)  86.6 us
    reduce_scatter x1, waiting for transfers between devices, shards(): lax.psum_scatter(head_term, 'fsdp', scatter_dimension=0, tiled=True)  73 us
    all_gather x1, waiting for transfers between devices, shards(): lax.all_gather(query_key_value_weight, 'fsdp', axis=0, tiled=True)  55.1 us
    all_gather x1, blocking collectives, shards(): full_head = lax.all_gather(head_weight, 'fsdp', axis=0, tiled=True)  46.6 us
  transfers between devices with their start and end apart: 10, of which 6 were waited for; matrix products, arithmetic and copies ran while one was open for 5% of the time, Pallas kernels for 0%

commit v1 on v0

--- a/solution.py
+++ b/solution.py
@@ -176,7 +176,7 @@
         hidden, grad_rows, (((0,), (0,)), ((), ())), preferred_element_type=jnp.float32
     )
     head_block = lax.psum_scatter(head_term, "fsdp", scatter_dimension=0, tiled=True)
-    grad_head = lax.psum(head_block, ("dp", "tile"))
+    grad_head = lax.psum(lax.psum(head_block, "dp"), "tile")
     grad_hidden = contract_last(grad_rows, full_head)
     grad_attended = contract_last(grad_hidden.astype(jnp.bfloat16), full_out).astype(jnp.bfloat16)
     grad_queries, pair_gradient_rows = attend_backward(

time: 945 us -> 548 us (0.58)
  the two profiles are of different devices: /device:TPU:2 before, /device:TPU:32 now
where the time goes in v1:
time: 548 us; the launch traced here: 547 us
  waiting for transfers between devices  370 us (68%)
  local copies, waits for them, and re-layouts  43.4 us (8%)
  blocking collectives  41.2 us (8%)
  matrix products  39.1 us (7%)
  starting transfers between devices  27.8 us (5%)
  between operations  14.1 us (3%)
  other arithmetic  11.4 us (2%)
    psum x2, waiting for transfers between devices, shards(): grad_head = lax.psum(lax.psum(head_block, 'dp'), 'tile')  172 us
    all_gather x1, waiting for transfers between devices, shards(): full_out = lax.all_gather(out_weight, 'fsdp', axis=0, tiled=True)  83.2 us
    reduce_scatter x1, waiting for transfers between devices, shards(): lax.psum_scatter(head_term, 'fsdp', scatter_dimension=0, tiled=True)  56.7 us
    all_gather x1, waiting for transfers between devices, shards(): lax.all_gather(query_key_value_weight, 'fsdp', axis=0, tiled=True)  53.7 us
    all_gather x1, blocking collectives, shards(): full_head = lax.all_gather(head_weight, 'fsdp', axis=0, tiled=True)  41.2 us
    ppermute x2, starting transfers between devices, with_halo(): after = lax.ppermute(leading, axis, down)  12.4 us
    unnamed x58, local copies, waits for them, and re-layouts  12.2 us
    dot_general x3, matrix products, contract_last(): lax.dot_general(left_side, right_side, (((1,), (1,)), ((), ())), preferre...  11.7 us
  transfers between devices with their start and end apart: 11, of which 7 were waited for; matrix products, arithmetic and copies ran while one was open for 12% of the time, Pallas kernels for 0%

profile of v1, /device:TPU:32, one launch (start us, length us, event | category | flops | bytes accessed | tf_op | source)
XLA Modules:
  0.0 547.1 jit_solution(11208140094290061172)
XLA Ops:
  8.7 1.7 fusion.56
  10.4 3.4 collective-permute-start.2
  13.8 5.8 %collective-permute-start.3 = (f32[20,8,1]{2,1,0:T(8,128)}, f32[20,8,1]{2,1,0:T(8,128)}, u32[]{:S(2)}, u32[]{:S(2)}) collective-permute-start(f32[20,8,1]{2,1,0:T(8,128)} %get-tuple-element.12), channel_id=1, source_target_pairs={{1,0},{2,1},{3,2},{4,3},{5,4},{6,5},{7,6},{8,7},{9,8},{10,9},{11,1... | collective-permute-start | bytes 1928 | tf_op jit(solution)/shard_map/ppermute | solution.py:24
  19.6 1.3 convert_reduce_fusion
  22.0 1.5 copy.23
  25.2 41.2 %all_gather.11 = bf16[1536,320]{1,0:T(8,128)(2,1)S(1)} all-gather(bf16[96,320]{1,0:T(8,128)(2,1)} %param.11), channel_id=1, replica_groups=mesh['dp'=2,'fsdp'=16,'tile'=16] {'fsdp'}, dimensions={0}, use_global_device_ids=true | all-gather | bytes 1044480 | tf_op jit(solution)/shard_map/all_gather | solution.py:144
  66.4 1.6 fusion.59
  68.0 1.2 multiply_convert_fusion.1
  69.8 2.1 convolution_bitcast_fusion.1
  72.0 53.7 %all-gather.3.cloned.1.call-done = bf16[1536,2304]{1,0:T(8,128)(2,1)} async-done(((bf16[96,2304]{1,0:T(8,128)(2,1)}), bf16[1536,2304]{1,0:T(8,128)(2,1)}) %all-gather.3.cloned.1.call-update) | async-done | bytes 7077904 | tf_op jit(solution)/shard_map/all_gather | solution.py:132
  125.7 5.3 convolution_convert_fusion
  132.7 2.5 collective-permute-start
  135.3 6.6 %collective-permute-start.1 = (bf16[8,8,1536]{2,1,0:T(8,128)(2,1)}, bf16[8,8,1536]{2,1,0:T(8,128)(2,1)}, u32[]{:S(2)}, u32[]{:S(2)}) collective-permute-start(bf16[8,8,1536]{2,1,0:T(8,128)(2,1)} %get-tuple-element.10), channel_id=1, source_target_pairs={{1,0},{2,1},{3,2},{4,3},{5,4},{6,5},{7,6},{8,7},{9,8},{10,9},{11,1... | collective-permute-start | bytes 589832 | tf_op jit(solution)/shard_map/ppermute | solution.py:24
  141.9 83.2 %all-gather.5.cloned.1.call-done = bf16[768,1536]{1,0:T(8,128)(2,1)} async-done(((bf16[48,1536]{1,0:T(8,128)(2,1)}), bf16[768,1536]{1,0:T(8,128)(2,1)}) %all-gather.5.cloned.1.call-update) | async-done | bytes 2359312 | tf_op jit(solution)/shard_map/all_gather | solution.py:141
  225.1 3.3 convolution_convert_fusion.1
  228.4 1.9 copy.24
  230.3 1.8 slice.50
  232.1 1.9 copy.18
  234.0 1.4 pad_maximum_fusion
  236.5 2.1 copy.29
  238.6 2.2 copy.28
  240.8 4.0 fusion.57
  244.8 2.9 convolution_convert_fusion.2
  247.9 1.6 convolution_bitcast_fusion
  251.6 2.1 fusion.60
  253.9 2.4 fusion.58
  256.3 2.4 reshape.187
  258.7 3.1 copy.20
  261.8 3.1 copy.21
  264.8 1.6 copy.26
  266.5 2.8 concatenate.20
  269.3 3.0 multiply_reduce_fusion
  273.0 1.1 copy-done.1
  274.6 1.7 copy.25
  276.3 1.9 concatenate.19
  279.6 1.5 copy-done.7
  282.0 2.5 collective-permute-start.4
  284.5 6.7 %collective-permute-start.5 = (f32[8,8,1536]{2,1,0:T(8,128)}, f32[8,8,1536]{2,1,0:T(8,128)}, u32[]{:S(2)}, u32[]{:S(2)}) collective-permute-start(f32[8,8,1536]{2,1,0:T(8,128)} %get-tuple-element.6), channel_id=1, source_target_pairs={{0,15},{1,0},{2,1},{3,2},{4,3},{5,4},{6,5},{7,6},{8,7},{9,8},{10,9... | collective-permute-start | bytes 1179656 | tf_op jit(solution)/shard_map/ppermute | solution.py:32
  292.9 2.2 fusion.11
  295.1 1.5 collective-permute-done.4
  296.6 1.2 collective-permute-done.5
  297.9 1.7 fusion.6
  299.6 6.9 %fusion.52 = (f32[256]{0:T(256)}, f32[256]{0:T(256)}, f32[256,1536]{1,0:T(8,128)}) fusion(f32[256]{0:T(256)S(1)} %rsqrt.12, f32[256]{0:T(256)S(1)} %div.51, bf16[1,8,32,1536]{3,2,1,0:T(8,128)(2,1)S(1)} %copy-done, f32[1536]{0:T(1024)S(1)} %copy-done.22, bf16[1536,2304]{1,0:T(8,128)(2,1)} %all-gather.3.cloned.1.call-done, ...), kind=kOutput, calls=%fused_computation.104 | convolution fusion | flops 1817050624 | bytes 10627072 | tf_op jit(solution)/shard_map/dot_general | solution.py:120
  306.5 56.7 %reduce-scatter.2.cloned.1.call-done = f32[96,320]{1,0:T(8,128)} async-done(((f32[1536,320]{1,0:T(8,128)}), f32[96,320]{1,0:T(8,128)}) %reduce-scatter.2.cloned.1.call-update) | async-done | bytes 122896 | tf_op jit(solution)/shard_map/reduce_scatter | solution.py:178
  364.0 62.1 %all-reduce.5.cloned.1.call-done = f32[96,320]{1,0:T(8,128)} async-done(((f32[96,320]{1,0:T(8,128)}), f32[96,320]{1,0:T(8,128)}) %all-reduce.5.cloned.1.call-update) | async-done | bytes 122896 | tf_op jit(solution)/shard_map/psum | solution.py:179
  426.0 2.9 add_convert_fusion
  428.9 110.1 %all-reduce.7.cloned.1.call-done = f32[96,320]{1,0:T(8,128)} async-done(((f32[96,320]{1,0:T(8,128)}), f32[96,320]{1,0:T(8,128)}) %all-reduce.7.cloned.1.call-update) | async-done | bytes 122896 | tf_op jit(solution)/shard_map/psum | solution.py:179
  539.0 1.6 copy.33
  (90 shorter events, 16.2 us)
Async XLA Ops:
  7.2 13.8 %copy-start = (bf16[1,8,32,1536]{3,2,1,0:T(8,128)(2,1)S(1)}, bf16[1,8,32,1536]{3,2,1,0:T(8,128)(2,1)}, u32[]{:S(2)}) copy-start(bf16[1,8,32,1536]{3,2,1,0:T(8,128)(2,1)} %param.7) | copy-start | bytes 2359300
  7.2 14.2 %copy-start.20 = (f32[1,20,32,128]{3,2,1,0:T(8,128)S(1)}, f32[1,20,32,128]{3,2,1,0:T(8,128)}, u32[]{:S(2)}) copy-start(f32[1,20,32,128]{3,2,1,0:T(8,128)} %param.13) | copy-start | bytes 983044
  7.2 118.5 %all-gather.3.cloned.1.call-start = ((), (), s32[]{:S(2)}) async-start(), calls=%async_computation.1 | async-start | bytes 7520256 | tf_op jit(solution)/shard_map/all_gather | solution.py:132
  7.9 217.2 %all-gather.5.cloned.1.call-start = ((), (), s32[]{:S(2)}) async-start(), calls=%async_computation.2 | async-start | bytes 2506752 | tf_op jit(solution)/shard_map/all_gather | solution.py:141
  8.7 354.5 %reduce-scatter.2.cloned.1.call-start = ((), (), s32[]{:S(2)}) async-start(), calls=%async_computation.3 | async-start | bytes 2506752 | tf_op jit(solution)/shard_map/reduce_scatter | solution.py:178
  10.4 59.4 %collective-permute-start.2 = (f32[20,8,1]{2,1,0:T(8,128)}, f32[20,8,1]{2,1,0:T(8,128)}, u32[]{:S(2)}, u32[]{:S(2)}) collective-permute-start(f32[20,8,1]{2,1,0:T(8,128)} %get-tuple-element.11), channel_id=1, source_target_pairs={{0,1},{1,2},{2,3},{3,4},{4,5},{5,6},{6,7},{7,8},{8,9},{9,10},{10,1... | collective-permute-start | bytes 1928 | tf_op jit(solution)/shard_map/ppermute | solution.py:23
  13.8 56.0 %collective-permute-start.3 = (f32[20,8,1]{2,1,0:T(8,128)}, f32[20,8,1]{2,1,0:T(8,128)}, u32[]{:S(2)}, u32[]{:S(2)}) collective-permute-start(f32[20,8,1]{2,1,0:T(8,128)} %get-tuple-element.12), channel_id=1, source_target_pairs={{1,0},{2,1},{3,2},{4,3},{5,4},{6,5},{7,6},{8,7},{9,8},{10,9},{11,1... | collective-permute-start | bytes 1928 | tf_op jit(solution)/shard_map/ppermute | solution.py:24
  66.4 1.6 copy-start.21
  66.4 3.4 copy-start.15
  130.9 1.8 copy-start.13
  131.0 0.9 copy-start.9
  132.7 101.3 %collective-permute-start = (bf16[8,8,1536]{2,1,0:T(8,128)(2,1)}, bf16[8,8,1536]{2,1,0:T(8,128)(2,1)}, u32[]{:S(2)}, u32[]{:S(2)}) collective-permute-start(bf16[8,8,1536]{2,1,0:T(8,128)(2,1)} %get-tuple-element.9), channel_id=1, source_target_pairs={{0,1},{1,2},{2,3},{3,4},{4,5},{5,6},{6,7},{7,8},{8,9},{9,10},{10,1... | collective-permute-start | bytes 589832 | tf_op jit(solution)/shard_map/ppermute | solution.py:23
  135.3 98.7 %collective-permute-start.1 = (bf16[8,8,1536]{2,1,0:T(8,128)(2,1)}, bf16[8,8,1536]{2,1,0:T(8,128)(2,1)}, u32[]{:S(2)}, u32[]{:S(2)}) collective-permute-start(bf16[8,8,1536]{2,1,0:T(8,128)(2,1)} %get-tuple-element.10), channel_id=1, source_target_pairs={{1,0},{2,1},{3,2},{4,3},{5,4},{6,5},{7,6},{8,7},{9,8},{10,9},{11,1... | collective-permute-start | bytes 589832 | tf_op jit(solution)/shard_map/ppermute | solution.py:24
  244.8 3.0 copy-start.3
  244.8 3.1 copy-start.17
  247.9 2.0 copy-start.5
  249.9 1.7 copy-start.12
  250.7 0.9 copy-start.6
  253.7 172.4 %all-reduce.5.cloned.1.call-start = ((), (), s32[]{:S(2)}) async-start(), calls=%async_computation.4 | async-start | bytes 294912 | tf_op jit(solution)/shard_map/psum | solution.py:179
  261.7 3.1 copy-start.14
  266.5 2.8 copy-start.16
  266.5 2.8 copy-start.18
  269.3 3.0 copy-start.4
  272.3 1.9 copy-start.11
  273.0 1.2 copy-start.1
  278.2 1.3 copy-start.10
  279.4 11.8 %copy-start.2 = (bf16[8,256,384]{2,1,0:T(8,128)(2,1)S(1)}, bf16[8,256,384]{2,1,0:T(8,128)(2,1)}, u32[]{:S(2)}) copy-start(bf16[8,256,384]{2,1,0:T(8,128)(2,1)} %copy-done.1) | copy-start | bytes 4718596
  279.4 11.8 %copy-start.8 = (bf16[384,768]{0,1:T(8,128)(2,1)S(1)}, bf16[384,768]{0,1:T(8,128)(2,1)}, u32[]{:S(2)}) copy-start(bf16[384,768]{0,1:T(8,128)(2,1)} %copy.29) | copy-start | bytes 1769476
  279.6 1.5 copy-start.7
  282.0 14.6 %collective-permute-start.4 = (f32[8,8,1536]{2,1,0:T(8,128)}, f32[8,8,1536]{2,1,0:T(8,128)}, u32[]{:S(2)}, u32[]{:S(2)}) collective-permute-start(f32[8,8,1536]{2,1,0:T(8,128)} %get-tuple-element.5), channel_id=1, source_target_pairs={{0,1},{1,2},{2,3},{3,4},{4,5},{5,6},{6,7},{7,8},{8,9},{9,10},{10,1... | collective-permute-start | bytes 1179656 | tf_op jit(solution)/shard_map/ppermute | solution.py:32
  284.5 8.4 %copy-start.23 = (s32[128]{0:T(128)S(1)}, s32[128]{0:T(128)}, u32[]{:S(2)}) copy-start(s32[128]{0:T(128)} %get-tuple-element.24) | copy-start | bytes 1540
  284.5 8.4 %copy-start.24 = (s32[128]{0:T(128)S(1)}, s32[128]{0:T(128)}, u32[]{:S(2)}) copy-start(s32[128]{0:T(128)} %get-tuple-element.25) | copy-start | bytes 1540
  284.5 8.4 %copy-start.25 = (f32[128]{0:T(128)S(1)}, f32[128]{0:T(128)}, u32[]{:S(2)}) copy-start(f32[128]{0:T(128)} %get-tuple-element.22) | copy-start | bytes 1540
  284.5 8.3 %copy-start.26 = (f32[128]{0:T(128)S(1)}, f32[128]{0:T(128)}, u32[]{:S(2)}) copy-start(f32[128]{0:T(128)} %get-tuple-element.23) | copy-start | bytes 1540
  284.5 13.3 %collective-permute-start.5 = (f32[8,8,1536]{2,1,0:T(8,128)}, f32[8,8,1536]{2,1,0:T(8,128)}, u32[]{:S(2)}, u32[]{:S(2)}) collective-permute-start(f32[8,8,1536]{2,1,0:T(8,128)} %get-tuple-element.6), channel_id=1, source_target_pairs={{0,15},{1,0},{2,1},{3,2},{4,3},{5,4},{6,5},{7,6},{8,7},{9,8},{10,9... | collective-permute-start | bytes 1179656 | tf_op jit(solution)/shard_map/ppermute | solution.py:32
  295.1 4.5 copy-start.19
  295.1 4.5 copy-start.22
  363.2 175.8 %all-reduce.7.cloned.1.call-start = ((), (), s32[]{:S(2)}) async-start(), calls=%async_computation.5 | async-start | bytes 294912 | tf_op jit(solution)/shard_map/psum | solution.py:179
Sparse Core Ops, SparseCore 0:
  10.1 115.5 all-gather.2
  127.7 97.3 all-gather.4
  253.8 109.3 reduce-scatter.1
  365.9 60.0 all-reduce.4
  429.1 109.8 all-reduce.6
